TPU v7x, 512 devices: a whole 4x8x8 slice. The times are simulated.
512 devices in a mesh: seq: 32 (over y, x), head: 16 (over z, core).
Axes of the slice: x: 4, y: 8, z: 8, core: 2. Of those that a mesh axis runs over, the one named last changes fastest.
Arguments:
- inputs: bfloat16 [16384, 4096], P('seq', 'head'), may hold values from -6 to 6
- gate: bfloat16 [16384, 4096], P('seq', 'head'), may hold values from -6 to 6
- input_map: bfloat16 [128, 16384], P('head', 'seq'), may hold values from -3 to 3
- output_map: bfloat16 [128, 16384], P('head', 'seq'), may hold values from -3 to 3
- step: float32 [64, 16384], P('head', 'seq'), may hold values from 0.25 to 2
- decay_rate: float32 [64], P('head'), may hold values from 3e-05 to 0.03
- level_mix: float32 [9, 64, 16384], P(None, 'head', 'seq'), may hold values from 0.1 to 1
- skip: float32 [64], P('head'), may hold values from 0.25 to 0.75
- norm_gain: float32 [4096], P('head'), may hold values from 0.5 to 1.5
Outputs:
- normed: bfloat16 [16384, 4096], P('seq', 'head')
All inputs are finite; a program needn't handle non-finite values.
Results may differ from a plain program's by a relative error of at most 0.0075.
Values may be sent and summed in bfloat16 or wider, within the bound.
A program may use at most 64 MiB of HBM per device.

v0:
```python
import jax
import jax.numpy as jnp
import numpy as np
from jax import lax
from jax.sharding import PartitionSpec as P

HEADS = 64
P_SIZE = 64
N = 128
GROUP = 256
LEVELS = 9


def span_table(groups, group_bits):
    table = np.zeros((groups, max(group_bits, 1), groups), np.float32)
    for later in range(groups):
        if later >> 0 & 1:
            for earlier in range(groups):
                if earlier >> 0 == (later >> 0) - 1:
                    table[later, 0, earlier] = 1.0
    return table


def to_rows(array):
    return jnp.transpose(array, (1, 2, 0))[..., None]


def project_states(out_blocks, states):
    groups, levels, heads_here, width, size = states.shape
    flat = jnp.transpose(states, (0, 3, 1, 2, 4)).reshape(groups, width, levels * heads_here * size)
    high = flat.astype(jnp.bfloat16)
    low = (flat - high.astype(jnp.float32)).astype(jnp.bfloat16)
    paired = jnp.concatenate([high, low], axis=2)
    proj = jnp.einsum("nct,cnk->ctk", out_blocks, paired, preferred_element_type=jnp.float32)
    half = levels * heads_here * size
    proj = proj[:, :, :half] + proj[:, :, half:]
    return proj.reshape(groups, out_blocks.shape[2], levels, heads_here, size)


def on_device(inputs, gate, input_map, output_map, step, decay_rate, level_mix, skip, norm_gain):
    highest = lax.Precision.HIGHEST
    tokens = inputs.shape[0]
    heads_here = inputs.shape[1] // P_SIZE
    groups = tokens // GROUP
    group_bits = groups.bit_length() - 1
    in_map, out_map = (
        lax.all_gather(input_map, "head", axis=0, tiled=True),
        lax.all_gather(output_map, "head", axis=0, tiled=True),
    )
    log_decay = -step * decay_rate[:, None]
    step_blocks = step.reshape(heads_here, groups, GROUP)
    cum = jnp.cumsum(log_decay.reshape(heads_here, groups, GROUP), axis=2)
    in_blocks = in_map.reshape(N, groups, GROUP)
    out_blocks = out_map.reshape(N, groups, GROUP)
    values = inputs.reshape(groups, GROUP, heads_here, P_SIZE)
    scores = jnp.einsum("nct,ncs->cts", out_blocks, in_blocks, preferred_element_type=jnp.float32)
    rows = jnp.arange(GROUP, dtype=jnp.int32)
    causal = (rows[:, None] >= rows[None, :])[None, None]
    spread = cum[:, :, :, None] - cum[:, :, None, :]
    within = jnp.where(causal, jnp.exp(jnp.where(causal, spread, 0.0)), 0.0)
    weights = (scores[None] * within * step_blocks[:, :, None, :]).astype(jnp.bfloat16)
    intra = jnp.einsum("hcts,cshp->cthp", weights, values, preferred_element_type=jnp.float32)
    to_end = jnp.exp(cum[:, :, -1:] - cum) * step_blocks
    loads = (in_blocks[None] * to_end[:, None]).astype(jnp.bfloat16)
    group_states = jnp.einsum("hncs,cshp->chnp", loads, values, preferred_element_type=jnp.float32)
    totals = cum[:, :, -1]
    after = jnp.cumsum(totals, axis=1)
    before = after - totals
    mixed = level_mix.reshape(LEVELS, heads_here, groups, GROUP)
    local_spans = None
    member = jnp.asarray(span_table(groups, group_bits))[None] > 0.5
    gap = before[:, :, None, None] - after[:, None, None, :]
    mixing = jnp.where(member, jnp.exp(jnp.where(member, gap, 0.0)), 0.0)
    local_spans = jnp.einsum("hjbk,khnp->jbhnp", mixing, group_states, precision=highest)
    shard_state = jnp.einsum(
        "hk,khnp->hnp", jnp.exp(after[:, -1:] - after), group_states, precision=highest
    )
    shard_total = after[:, -1]
    rank = lax.axis_index("seq")
    seq_bits = lax.axis_size("seq").bit_length() - 1
    totals_all = lax.all_gather(shard_total[None], "seq", axis=0, tiled=True)
    ends = jnp.cumsum(totals_all, axis=0)
    starts = ends - totals_all
    mine = lax.dynamic_slice_in_dim(starts, rank, 1, 0)
    piece = lax.all_gather(shard_state[None], "seq", axis=0, tiled=True)
    count = piece.shape[0]
    index = jnp.arange(count, dtype=jnp.int32)
    flipped = jnp.bitwise_xor(index, rank)
    levels = jnp.stack([jnp.right_shift(flipped, level) == 1 for level in range(seq_bits)], axis=1)
    valid = (index < rank)[:, None]
    gap = mine - ends
    weight = jnp.where(valid, jnp.exp(jnp.where(valid, gap, 0.0)), 0.0)
    far_spans = jnp.einsum(
        "kb,kh,khnp->bhnp", levels.astype(jnp.float32), weight, piece, precision=highest
    )
    far_wide = jnp.broadcast_to(far_spans[None], (groups, seq_bits, heads_here, N, P_SIZE))
    all_states = jnp.concatenate([local_spans, far_wide], axis=1)
    proj = project_states(out_blocks, all_states)
    level = 0
    near = to_rows(mixed[1 + level]) * proj[:, :, level]
    far = jnp.zeros((groups, GROUP, heads_here, P_SIZE), jnp.float32)
    for level in range(seq_bits):
        far = far + to_rows(mixed[1 + group_bits + level]) * proj[:, :, group_bits + level]
    total = to_rows(mixed[0]) * intra
    total = total + to_rows(jnp.exp(cum)) * near
    total = total + to_rows(jnp.exp(cum + before[:, :, None])) * far
    total = total + skip[None, None, :, None] * values.astype(jnp.float32)
    gated = total.reshape(tokens, heads_here * P_SIZE) * jax.nn.silu(gate.astype(jnp.float32))
    squares = jnp.sum(gated * gated, axis=1)
    summed = lax.psum(squares, "head")
    scale = lax.rsqrt(summed / (HEADS * P_SIZE) + 1e-05)
    return (gated * scale[:, None] * norm_gain[None, :]).astype(jnp.bfloat16)


def solution(mesh):
    return jax.shard_map(
        on_device,
        mesh=mesh,
        in_specs=(
            P("seq", "head"),
            P("seq", "head"),
            P("head", "seq"),
            P("head", "seq"),
            P("head", "seq"),
            P("head"),
            P(None, "head", "seq"),
            P("head"),
            P("head"),
        ),
        out_specs=P("seq", "head"),
        check_vma=False,
    )
```

profile of v0, /device:TPU:1, one launch (start us, length us, event | category | flops | bytes accessed | tf_op | source)
XLA Modules:
  0.0 175.5 jit_solution(9207128223247510060)
XLA Ops:
  6.5 0.8 negate_multiply_fusion
  7.3 2.4 %reduce-window.6 = f32[4,2,2,128]{3,2,1,0:T(2,128)S(1)} reduce-window(f32[4,2,2,128]{3,2,1,0:T(2,128)S(1)} %reshape.198, f32[]{:T(128)} %constant.14.clone.1), window={size=1x1x1x128 pad=0_0x0_0x0_0x127_0}, to_apply=%region_0.0 | reduce-window | flops 260096 | bytes 16388 | tf_op jit(solution)/shard_map/reduce-window
  9.8 0.1 copy.157
  10.5 0.7 mul.157
  11.4 1.2 reshape.216
  12.6 0.3 copy.163
  12.9 25.2 %all_gather.13 = bf16[128,512]{1,0:T(8,128)(2,1)S(1)} all-gather(bf16[8,512]{1,0:T(8,128)(2,1)} %param.12), channel_id=1, replica_groups=mesh['seq'=32,'head'=16] {'head'}, dimensions={0}, use_global_device_ids=true | all-gather | bytes 139264 | tf_op jit(solution)/shard_map/all_gather | solution.py:47
  38.1 0.1 copy.155
  38.2 0.1 copy.166
  38.3 1.0 multiply_reduce_fusion.1
  39.4 1.3 dynamic-slice
  41.4 61.7 %all-reduce = f32[128]{0:T(128)S(1)} all-reduce(f32[128]{0:T(128)S(1)} %fusion.51), channel_id=2, replica_groups=mesh['seq'=32,'head'=16] {'seq'}, use_global_device_ids=true, to_apply=%add | all-reduce | flops 128 | bytes 1024
  103.4 1.1 convolution_bitcast_fusion.2
  104.5 28.7 %all_gather.12 = bf16[128,512]{1,0:T(8,128)(2,1)S(1)} all-gather(bf16[8,512]{1,0:T(8,128)(2,1)S(1)} %copy-done.3), channel_id=1, replica_groups=mesh['seq'=32,'head'=16] {'head'}, dimensions={0}, use_global_device_ids=true | all-gather | bytes 139264 | tf_op jit(solution)/shard_map/all_gather | solution.py:48
  133.2 0.1 copy.154
  133.3 0.1 copy.192
  133.8 0.2 fusion.53
  134.1 2.5 %broadcast_multiply_fusion = f32[32,4,128,64]{2,3,1,0:T(8,128)S(1)} fusion(f32[32,4,128,64]{2,3,1,0:T(8,128)} %bitcast.154, f32[32,4]{1,0:T(8,128)S(1)} %exponential_select_fusion), kind=kLoop, calls=%fused_computation.4 | loop fusion | flops 1048576 | bytes 8389120 | tf_op jit(solution)/shard_map/kb,kh,khnp->bhnp/dot_general | solution.py:93
  136.6 3.8 %fusion = f32[5,4,128,64]{2,0,3,1:T(8,128)S(1)} fusion(f32[32,4,128,64]{2,3,1,0:T(8,128)S(1)} %broadcast_multiply_fusion, pred[32,5]{0,1:T(8,128)(4,1)S(1)} %stack.2), kind=kOutput, calls=%fused_computation.1 | convolution fusion | flops 62914560 | bytes 4849824 | tf_op jit(solution)/shard_map/kb,kh,khnp->bhnp/dot_general | solution.py:93
  140.5 0.1 copy.175
  140.6 0.1 broadcast_in_dim.91
  140.7 0.2 pad_maximum_fusion
  140.9 0.2 fusion.5
  141.1 1.0 convolution_bitcast_fusion
  142.1 0.4 slice_add_fusion
  142.5 0.3 copy-done.2
  142.8 1.0 fusion.9
  143.9 0.4 copy.191
  144.3 0.2 multiply_reduce_fusion
  144.5 23.1 %psum.7 = f32[512]{0:T(512)S(1)} all-reduce(f32[512]{0:T(512)S(1)} %multiply_reduce_fusion), channel_id=1, replica_groups=mesh['seq'=32,'head'=16] {'head'}, use_global_device_ids=true, to_apply=%region_5.6 | all-reduce | flops 512 | bytes 4096 | tf_op jit(solution)/shard_map/psum | solution.py:110
  167.6 0.2 multiply_convert_fusion.4
  167.8 0.8 copy.193
  (51 shorter events, 1.6 us)
Async XLA Ops:
  6.5 96.8 %copy-start.6 = (pred[2,2]{1,0:T(4,128)(4,1)S(1)}, pred[2,2]{1,0:T(4,128)(4,1)}, u32[]{:S(2)}) copy-start(pred[2,2]{1,0:T(4,128)(4,1)} %constant.50) | copy-start | bytes 16
  6.5 127.5 %all-gather.4.cloned.1.call-start = ((), (), s32[]{:S(2)}) async-start(), calls=%async_computation | async-start | bytes 4325376 | tf_op jit(solution)/shard_map/all_gather | solution.py:85
  11.3 93.2 %copy-start.3 = (bf16[8,512]{1,0:T(8,128)(2,1)S(1)}, bf16[8,512]{1,0:T(8,128)(2,1)}, u32[]{:S(2)}) copy-start(bf16[8,512]{1,0:T(8,128)(2,1)} %param.13) | copy-start | bytes 24580
  12.6 120.7 %copy-start = (bf16[512,256]{1,0:T(8,128)(2,1)S(1)}, bf16[512,256]{1,0:T(8,128)(2,1)}, u32[]{:S(2)}) copy-start(bf16[512,256]{1,0:T(8,128)(2,1)} %param.11) | copy-start | bytes 786436
  12.9 120.9 %copy-start.1 = (f32[9,4,512]{2,1,0:T(4,128)S(1)}, f32[9,4,512]{2,1,0:T(4,128)}, u32[]{:S(2)}) copy-start(f32[9,4,512]{2,1,0:T(4,128)} %param.16) | copy-start | bytes 221188
  142.1 0.7 copy-start.2
  142.1 0.7 copy-start.5
  143.8 23.7 %copy-start.4 = (f32[256]{0:T(256)S(1)}, f32[256]{0:T(256)}, u32[]{:S(2)}) copy-start(f32[256]{0:T(256)} %param.18) | copy-start | bytes 3076
Sparse Core Ops, SparseCore 0:
  39.5 80.0 all-gather.3
where the time goes:
time: 176 us; the launch traced here: 175 us
  blocking collectives  139 us (79%)
  between operations  14.3 us (8%)
  matrix products  8.16 us (5%)
  other arithmetic  7.43 us (4%)
  local copies, waits for them, and re-layouts  6.88 us (4%)
    unnamed x1, blocking collectives  61.7 us
    all_gather x1, blocking collectives, on_device(): lax.all_gather(output_map, 'head', axis=0, tiled=True)  28.7 us
    all_gather x1, blocking collectives, on_device(): lax.all_gather(input_map, 'head', axis=0, tiled=True)  25.2 us
    psum x1, blocking collectives, on_device(): summed = lax.psum(squares, 'head')  23.1 us
    dot_general x1, matrix products, on_device(): jnp.einsum('kb,kh,khnp->bhnp', levels.astype(jnp.float32), weight, piece,...  3.83 us
  transfers between devices with their start and end apart: 1, of which 0 were waited for; matrix products, arithmetic and copies ran while one was open for 2% of the time, Pallas kernels for 0%

commit v1 on v0

v1 whole, which is shorter than its diff:
```python
import functools

import jax
import jax.numpy as jnp
from jax import lax
from jax.experimental import pallas as pl
from jax.experimental.pallas import tpu as pltpu
from jax.sharding import PartitionSpec as P

P_SIZE = 64
N = 128
GROUP = 256
EPS = 1e-05
X = 4
F32, BF16 = jnp.float32, jnp.bfloat16
MESH = pl.DeviceIdType.MESH


def ring_offsets(chips):
    order = []
    for far in range(chips // 2, 0, -1):
        ways = (far,) if 2 * far == chips else (far, chips - far)
        order += [(way, flip) for flip in (0, 1) for way in ways]
    return order + [(0, 1)]


def iota(shape, dim):
    return lax.broadcasted_iota(jnp.int32, shape, dim)


def dot(a, b):
    return jnp.dot(a, b, preferred_element_type=F32)


def split_rows(v):
    high = v.astype(BF16).astype(F32)
    return jnp.where(iota(v.shape, 0) < 4, high, v - high)


def lanes(tile):
    low = iota((1, 128), 1) < P_SIZE
    return jnp.concatenate(
        [jnp.where(low, tile[0:1], tile[1:2]), jnp.where(low, tile[2:3], tile[3:4])], axis=1
    )


def kernel(
    rows_y, chips_z,
    x_hbm, gate_hbm, b_ref, c_ref, step_ref, rate_ref, mix_hbm, skip_ref, gain_ref,
    out_ref,
    x_ref, gate_ref, mix_ref, b_all, c_all, drive, factor, silu, pre, gated, ct_ref,
    state, piece, row_state, tot, row_tot, row_sum, row_in, span, squares,
    near_state,
    local_sem, z_send, z_recv, x_send, x_recv, y_send, y_recv,
):
    shard, col = lax.axis_index("seq"), lax.axis_index("head")
    y, x = shard // X, shard % X
    z, core = col // 2, col % 2
    heads = 2 * chips_z
    own = b_ref.shape[0]
    cut = N // X
    bits_y = rows_y.bit_length() - 1
    offsets = ring_offsets(chips_z)

    def z_peer(offset):
        way, flip = offset
        return ((z + way) % chips_z) * 2 + (core + flip) % 2

    def z_copy(kind, slot, src, dst):
        return pltpu.make_async_remote_copy(
            src_ref=src, dst_ref=dst, send_sem=z_send.at[kind, slot], recv_sem=z_recv.at[kind, slot],
            device_id=(shard, z_peer(offsets[slot])), device_id_type=MESH,
        )

    def x_copy(kind, ahead, src, dst):
        return pltpu.make_async_remote_copy(
            src_ref=src, dst_ref=dst, send_sem=x_send.at[kind, ahead], recv_sem=x_recv.at[kind, ahead],
            device_id=(y * X + (x + ahead) % X, col), device_id_type=MESH,
        )

    def y_copy(kind, ahead, src, dst):
        return pltpu.make_async_remote_copy(
            src_ref=src, dst_ref=dst, send_sem=y_send.at[kind, ahead], recv_sem=y_recv.at[kind, ahead],
            device_id=(((y + ahead) % rows_y) * X + x, col), device_id_type=MESH,
        )

    barrier = pltpu.get_barrier_semaphore()
    for offset in offsets:
        pl.semaphore_signal(barrier, inc=1, device_id=(shard, z_peer(offset)), device_id_type=MESH)
    for ahead in range(1, X):
        pl.semaphore_signal(
            barrier, inc=1, device_id=(y * X + (x + ahead) % X, col), device_id_type=MESH
        )
    for ahead in range(1, rows_y):
        pl.semaphore_signal(
            barrier, inc=1, device_id=(((y + ahead) % rows_y) * X + x, col), device_id_type=MESH
        )

    mine = pl.ds(pl.multiple_of(col * own, own), own)
    loads = [
        pltpu.make_async_copy(x_hbm, x_ref, local_sem.at[0]),
        pltpu.make_async_copy(mix_hbm, mix_ref, local_sem.at[1]),
        pltpu.make_async_copy(gate_hbm, gate_ref, local_sem.at[2]),
        pltpu.make_async_copy(b_ref, b_all.at[mine], local_sem.at[3]),
        pltpu.make_async_copy(c_ref, c_all.at[mine], local_sem.at[4]),
    ]
    for load in loads:
        load.start()

    rate = jnp.zeros((8, 1), F32)
    skip = jnp.zeros((1, 256), F32)
    for head in range(4):
        rate = jnp.where(iota((8, 1), 0) % 4 == head, rate_ref[head], rate)
        skip = jnp.where(iota((1, 256), 1) // P_SIZE == head, skip_ref[head], skip)
    step = jnp.concatenate([step_ref[...], step_ref[...]], axis=0)
    log_decay = -step * rate
    parts = []
    for group in range(2):
        v = log_decay[:, group * GROUP : (group + 1) * GROUP]
        first = v.astype(BF16).astype(F32)
        second = (v - first).astype(BF16).astype(F32)
        parts += [first, second, v - first - second]
    upper = (iota((GROUP, GROUP), 0) <= iota((GROUP, GROUP), 1)).astype(F32).astype(BF16)
    sums = dot(jnp.concatenate(parts, axis=0).astype(BF16), upper)
    cum = [sums[g * 24 : g * 24 + 8] + sums[g * 24 + 8 : g * 24 + 16] + sums[g * 24 + 16 : g * 24 + 24] for g in range(2)]
    total_0, total_1 = (jnp.broadcast_to(c[:, GROUP - 1 :], (8, 128)) for c in cum)
    total = total_0 + total_1
    tot[x] = total
    both = jnp.concatenate(cum, axis=1)
    grow = jnp.exp(-both) * step
    decay = jnp.exp(both)
    far_decay = jnp.exp(jnp.concatenate([cum[0], cum[1] + cum[0][:, GROUP - 1 :]], axis=1))
    expander = (iota((8, 256), 0) % 4 == iota((8, 256), 1) // P_SIZE).astype(F32).astype(BF16)

    def expand(v):
        return dot(split_rows(v).T.astype(BF16), expander)

    loads[0].wait()
    drive[...] = (expand(grow) * x_ref[...].astype(F32)).astype(BF16)

    pl.semaphore_wait(barrier, heads - 1 + X - 1 + rows_y - 1)
    b_copies = [z_copy(0, s, b_ref, b_all.at[mine]) for s in range(heads - 1)]
    c_copies = [z_copy(1, s, c_ref, c_all.at[mine]) for s in range(heads - 1)]
    tot_copies = [x_copy(0, a, tot.at[x], tot.at[x]) for a in range(1, X)]
    for copy in b_copies + tot_copies + c_copies:
        copy.start()

    loads[1].wait()
    for level in range(4 + bits_y):
        mix = jnp.concatenate([mix_ref[level], mix_ref[level]], axis=0)
        factor[level] = expand(mix * (decay if level < 2 else far_decay))
    loads[2].wait()
    gate = gate_ref[...].astype(F32)
    silu[...] = gate / (1.0 + jnp.exp(-gate))

    for copy in tot_copies:
        copy.wait()
    totals = [tot[i] for i in range(X)]
    after = jnp.zeros((8, 128), F32)
    row_weight = [None] * X
    for i in reversed(range(X)):
        row_weight[i] = lanes(jnp.exp(after))
        after = after + totals[i]
    row_tot[y] = after
    row_copies = [y_copy(0, a, row_tot.at[y], row_tot.at[y]) for a in range(1, rows_y)]
    for a in range(1, rows_y):
        pl.when(y + a < rows_y)(row_copies[a - 1].start)
    before = jnp.zeros((8, 128), F32)
    for i in range(X):
        before = before + jnp.where(i < x, totals[i], 0.0)
    row_factor = lanes(jnp.exp(before))
    pair_last = jnp.where(x == 3, totals[2], 0.0)
    pair_weight = [lanes(jnp.exp(totals[1] + pair_last)), lanes(jnp.exp(pair_last))]

    loads[3].wait()
    for copy in b_copies:
        copy.wait_recv()
    state_0 = lanes(jnp.exp(total_0)) * dot(b_all[:, :GROUP], drive[:GROUP])
    state_1 = state_0 + dot(b_all[:, GROUP:], drive[GROUP:])
    state[...] = (lanes(jnp.exp(total_1)) * state_1).astype(BF16)
    near_state[...] = state_0.astype(BF16)
    piece_copies = [
        x_copy(1, a, state.at[pl.ds(pl.multiple_of((x + a) % X * cut, cut), cut)], piece.at[x])
        for a in range(1, X)
    ]
    state_copies = [x_copy(2, a, state, row_state.at[x]) for a in range(1, X)]
    for copy in piece_copies:
        copy.start()
    for a in range(1, X):
        pl.when(x + a < X)(state_copies[a - 1].start)
    own_cut = pl.ds(pl.multiple_of(x * cut, cut), cut)
    piece[x] = state[own_cut, :]

    loads[4].wait()
    for copy in c_copies:
        copy.wait_recv()
    ct_ref[...] = c_all[...].astype(F32).T.astype(BF16)

    for copy in piece_copies:
        copy.wait_recv()
    row = sum(row_weight[i] * piece[i].astype(F32) for i in range(X))
    row_sum[...] = row.astype(BF16)
    sum_copies = [y_copy(1, a, row_sum, row_in.at[y]) for a in range(1, rows_y)]
    for a in range(1, rows_y):
        pl.when(y + a < rows_y)(sum_copies[a - 1].start)

    causal = iota((GROUP, GROUP), 0) >= iota((GROUP, GROUP), 1)
    for group in range(2):
        rows = slice(group * GROUP, (group + 1) * GROUP)
        scores = dot(ct_ref[rows], b_all[:, rows])
        scores = jnp.where(causal, scores, 0.0).astype(BF16)
        acc = factor[0, rows] * dot(scores, drive[rows]) + skip * x_ref[rows].astype(F32)
        if group == 1:
            acc = acc + factor[1, rows] * dot(ct_ref[rows], near_state[...])
        pre[rows] = acc

    for a in range(1, X):
        pl.when(x - a >= 0)(state_copies[a - 1].wait_recv)

    @pl.when(x % 2 == 1)
    def _():
        pre[...] += factor[2] * dot(ct_ref[...], row_state[x - 1])

    @pl.when(x >= 2)
    def _():
        pair = pair_weight[0] * row_state[0].astype(F32) + pair_weight[1] * row_state[1].astype(F32)
        pre[...] += factor[3] * dot(ct_ref[...], pair.astype(BF16))

    for a in range(1, rows_y):
        pl.when(y - a >= 0)(row_copies[a - 1].wait_recv)
    gap = jnp.zeros((8, 128), F32)
    row_gap = [None] * rows_y
    for q in reversed(range(rows_y - 1)):
        row_gap[q] = lanes(jnp.exp(gap))
        gap = gap + jnp.where(q < y, row_tot[q], 0.0)
    for a in range(1, rows_y):
        pl.when(y - a >= 0)(sum_copies[a - 1].wait_recv)
    spans = [jnp.zeros((cut, 256), F32)] * bits_y
    for q in range(rows_y - 1):
        part = row_gap[q] * row_in[q].astype(F32)
        for bit in range(bits_y):
            hit = jnp.logical_and(q // 2 ** (bit + 1) == y // 2 ** (bit + 1), q // 2**bit < y // 2**bit)
            spans[bit] = spans[bit] + jnp.where(hit, part, 0.0)
    span[own_cut] = jnp.concatenate(spans, axis=1).astype(BF16)
    span_copies = [x_copy(3, a, span.at[own_cut], span.at[own_cut]) for a in range(1, X)]
    for copy in span_copies:
        copy.start()
    for copy in span_copies:
        copy.wait()

    ones = jnp.ones((8, 128), BF16)
    far = factor[4] * dot(ct_ref[...], span[:, :256])
    for bit in range(1, bits_y):
        far = far + factor[4 + bit] * dot(ct_ref[...], span[:, bit * 256 : (bit + 1) * 256])
    g = (pre[...] + row_factor * far) * silu[...]
    gg = g * g
    gg = gg[:, :128] + gg[:, 128:]
    high = gg.astype(BF16)
    low = (gg - high.astype(F32)).astype(BF16)
    flat = (((1,), (1,)), ((), ()))
    line = lax.dot_general(ones, high, flat, preferred_element_type=F32)
    line = line + lax.dot_general(ones, low, flat, preferred_element_type=F32)
    packed = jnp.concatenate([line[0:1, j * 128 : (j + 1) * 128] for j in range(4)], axis=0)
    squares[col] = packed
    square_copies = [z_copy(2, s, squares.at[col], squares.at[col]) for s in range(heads - 1)]
    for copy in square_copies:
        copy.start()
    gated[...] = g * gain_ref[...]

    for copy in b_copies + c_copies:
        copy.wait_send()
    for copy in piece_copies:
        copy.wait_send()
    for a in range(1, X):
        pl.when(x + a < X)(state_copies[a - 1].wait_send)
    for a in range(1, rows_y):
        pl.when(y + a < rows_y)(row_copies[a - 1].wait_send)
        pl.when(y + a < rows_y)(sum_copies[a - 1].wait_send)

    for copy in square_copies:
        copy.wait()
    summed = squares[0]
    for k in range(1, heads):
        summed = summed + squares[k]
    scale = lax.rsqrt(summed / (heads * 256) + EPS)
    scale = jnp.concatenate([jnp.broadcast_to(scale[j : j + 1], (8, 128)) for j in range(4)], axis=1)
    wide = dot((split_rows(scale) * 0.25).T.astype(BF16), ones)
    for half in range(2):
        cols = slice(half * 128, (half + 1) * 128)
        out_ref[:, cols] = (gated[:, cols] * wide).astype(BF16)


def on_device(rows_y, chips_z, inputs, gate, input_map, output_map, step, decay_rate, level_mix, skip, norm_gain):
    tokens, width = inputs.shape
    cut = N // X
    bits_y = rows_y.bit_length() - 1
    heads = 2 * chips_z
    vmem = pl.BlockSpec(memory_space=pltpu.VMEM)
    smem = pl.BlockSpec(memory_space=pltpu.SMEM)
    hbm = pl.BlockSpec(memory_space=pl.ANY)
    scratch = [
        pltpu.VMEM((tokens, width), BF16),
        pltpu.VMEM((tokens, width), BF16),
        pltpu.VMEM(level_mix.shape, F32),
        pltpu.VMEM((N, tokens), BF16),
        pltpu.VMEM((N, tokens), BF16),
        pltpu.VMEM((tokens, width), BF16),
        pltpu.VMEM((4 + bits_y, tokens, width), F32),
        pltpu.VMEM((tokens, width), F32),
        pltpu.VMEM((tokens, width), F32),
        pltpu.VMEM((tokens, width), F32),
        pltpu.VMEM((tokens, N), BF16),
        pltpu.VMEM((N, width), BF16),
        pltpu.VMEM((X, cut, width), BF16),
        pltpu.VMEM((X, N, width), BF16),
        pltpu.VMEM((X, 8, 128), F32),
        pltpu.VMEM((rows_y, 8, 128), F32),
        pltpu.VMEM((cut, width), BF16),
        pltpu.VMEM((rows_y, cut, width), BF16),
        pltpu.VMEM((N, bits_y * width), BF16),
        pltpu.VMEM((heads, 4, 128), F32),
        pltpu.VMEM((N, width), BF16),
        pltpu.SemaphoreType.DMA((5,)),
        pltpu.SemaphoreType.DMA((3, heads - 1)),
        pltpu.SemaphoreType.DMA((3, heads - 1)),
        pltpu.SemaphoreType.DMA((4, X)),
        pltpu.SemaphoreType.DMA((4, X)),
        pltpu.SemaphoreType.DMA((2, rows_y)),
        pltpu.SemaphoreType.DMA((2, rows_y)),
    ]
    return pl.pallas_call(
        functools.partial(kernel, rows_y, chips_z),
        out_shape=jax.ShapeDtypeStruct((tokens, width), BF16),
        in_specs=[hbm, hbm, vmem, vmem, vmem, smem, hbm, smem, vmem],
        out_specs=vmem,
        scratch_shapes=scratch,
        compiler_params=pltpu.CompilerParams(collective_id=0, has_side_effects=True),
    )(inputs, gate, input_map, output_map, step, decay_rate, level_mix, skip, norm_gain.reshape(1, width))


def solution(mesh):
    rows_y, chips_z = mesh.shape["seq"] // X, mesh.shape["head"] // 2
    return jax.shard_map(
        functools.partial(on_device, rows_y, chips_z),
        mesh=mesh,
        in_specs=(
            P("seq", "head"),
            P("seq", "head"),
            P("head", "seq"),
            P("head", "seq"),
            P("head", "seq"),
            P("head"),
            P(None, "head", "seq"),
            P("head"),
            P("head"),
        ),
        out_specs=P("seq", "head"),
        check_vma=False,
    )
```

time: 176 us -> 42.3 us (0.24)
  the two profiles are of different devices: /device:TPU:1 before, /device:TPU:57 now
where the time goes in v1:
time: 42.3 us; the launch traced here: 42.1 us
  Pallas kernels  40.5 us (96%)
  local copies, waits for them, and re-layouts  1.67 us (4%)
    pallas_call x1, Pallas kernels, on_device(): pl.pallas_call(functools.partial(kernel, rows_y, chips_z), out_shape=jax....  40.5 us
    unnamed x1, local copies, waits for them, and re-layouts  1.67 us

profile of v1, /device:TPU:57, one launch (start us, length us, event | category | flops | bytes accessed | tf_op | source)
XLA Modules:
  0.0 42.1 jit_solution(12188612941266348021)
XLA Ops:
  0.0 40.5 %shard_map.91 = bf16[512,256]{1,0:T(8,128)(2,1)} custom-call(bf16[512,256]{1,0:T(8,128)(2,1)} %x_hbm.1, bf16[512,256]{1,0:T(8,128)(2,1)} %gate_hbm.1, bf16[8,512]{1,0:T(8,128)(2,1)} %b_ref.1, bf16[8,512]{1,0:T(8,128)(2,1)} %c_ref.1, f32[4,512]{1,0:T(4,128)} %step_ref.1, f32[4]{0:T(128)} %rate_ref.1, f32[9,4,512]{2,1,0:T(4,128)} %mix_hbm.1, f32[4]{0:T(128)} %skip_ref.1, ...), custom_call_target="tpu_custom_call" | custom-call | tf_op jit(solution)/shard_map/pallas_call | solution.py:331
  40.5 1.7 %copy.11 = bf16[512,256]{1,0:T(8,128)(2,1)} copy(bf16[512,256]{1,0:T(8,128)(2,1)} %shard_map.91) | data formatting | bytes 524288
